TPU v7x, 32 devices: a whole 2x2x4 slice. The times are simulated.
32 devices in a mesh: dp: 2 (over y), fsdp: 16 (over z, x, core).
Axes of the slice: x: 2, y: 2, z: 4, core: 2. Of those that a mesh axis runs over, the one named last changes fastest.
Arguments:
- tokens: bfloat16 [65536, 768], P(('dp', 'fsdp')), may hold values from -12 to 12
- cotangent: bfloat16 [65536, 768], P(('dp', 'fsdp')), may hold values from -12 to 12
- segment_ids: int32 [65536], P(('dp', 'fsdp')), may hold values from 0 to 2687, as said below
- first_gain: bfloat16 [768], P('fsdp'), may hold values from 0.25 to 1.75
- first_shift: bfloat16 [768], P('fsdp'), may hold values from -1.75 to 1.75
- triple_weight: bfloat16 [768, 2304], P('fsdp'), may hold values from -0.3125 to 0.3125
- query_bias: bfloat16 [768], P('fsdp'), may hold values from -3 to 3
- value_bias: bfloat16 [768], P('fsdp'), may hold values from -1.75 to 1.75
- out_weight: bfloat16 [768, 768], P('fsdp'), may hold values from -0.875 to 0.875
- out_bias: bfloat16 [768], P('fsdp'), may hold values from -1.75 to 1.75
- second_gain: bfloat16 [768], P('fsdp'), may hold values from 0.25 to 1.75
- second_shift: bfloat16 [768], P('fsdp'), may hold values from -1.75 to 1.75
- up_weight: bfloat16 [768, 3072], P('fsdp'), may hold values from -0.21875 to 0.21875
- up_bias: bfloat16 [3072], P('fsdp'), may hold values from -3 to 3
- down_weight: bfloat16 [3072, 768], P('fsdp'), may hold values from -0.109375 to 0.109375
- down_bias: bfloat16 [768], P('fsdp'), may hold values from -1.75 to 1.75
Outputs:
- block_output: bfloat16 [65536, 768], P(('dp', 'fsdp'))
- tokens_gradient: bfloat16 [65536, 768], P(('dp', 'fsdp'))
- first_gain_gradient: float32 [768], P('fsdp')
- first_shift_gradient: float32 [768], P('fsdp')
- triple_weight_gradient: float32 [768, 2304], P('fsdp')
- query_bias_gradient: float32 [768], P('fsdp')
- value_bias_gradient: float32 [768], P('fsdp')
- out_weight_gradient: float32 [768, 768], P('fsdp')
- out_bias_gradient: float32 [768], P('fsdp')
- second_gain_gradient: float32 [768], P('fsdp')
- second_shift_gradient: float32 [768], P('fsdp')
- up_weight_gradient: float32 [768, 3072], P('fsdp')
- up_bias_gradient: float32 [3072], P('fsdp')
- down_weight_gradient: float32 [3072, 768], P('fsdp')
- down_bias_gradient: float32 [768], P('fsdp')
Inputs may be any that keep to these rules, and one draw needn't show every extreme that they name: `segment_ids`: segment numbers never fall along the patches and no image spans two aligned blocks of 1024 patches; each image has 900 patches and begins its block, or has 1 to 64 patches; the first block begins with an image of 900 patches; the last patch carries exactly the largest number, 65536 // 1024 * (1024 // max(1, 25) + 2) - 1.
All inputs are finite; a program needn't handle non-finite values.
Results may differ from a plain program's by a relative error of at most 0.014.
Values may be sent and summed in bfloat16 or wider, within the bound.
A program may use at most 384 MiB of HBM per device.

v0:
```python
import jax
import jax.numpy as jnp
from jax import lax
from jax.sharding import PartitionSpec as P

H = 12
HD = 64
ROWS = 1024
MB = 2
norm_eps = 1e-06
root_half = 0.7071067811865476
root_inv_two_pi = 0.3989422804014327


def norm_forward(values, gain, shift):
    mean_val = jnp.mean(values, axis=-1, keepdims=True)
    centered = values - mean_val
    variance = jnp.mean(centered * centered, axis=-1, keepdims=True)
    inv_std = lax.rsqrt(variance + norm_eps)
    normed = centered * inv_std
    return (normed * gain + shift, normed, inv_std)


def norm_backward(grad_out, normed, inv_std, gain):
    gain_part = jnp.sum(grad_out * normed, axis=0)
    shift_part = jnp.sum(grad_out, axis=0)
    grad_norm = grad_out * gain
    mean_plain = jnp.mean(grad_norm, axis=-1, keepdims=True)
    mean_cross = jnp.mean(grad_norm * normed, axis=-1, keepdims=True)
    return (inv_std * (grad_norm - mean_plain - normed * mean_cross), gain_part, shift_part)


def gelu_slope(upped):
    normal_cdf = 0.5 * (1.0 + lax.erf(upped * root_half))
    return normal_cdf + upped * jnp.exp(-0.5 * upped * upped) * root_inv_two_pi


def masked_scores(query_block, keys, seg_block, segments):
    scores = (
        jnp.einsum("qhd,khd->hqk", query_block, keys, preferred_element_type=jnp.float32) * 0.125
    )
    allowed = seg_block[:, None] == segments[None, :]
    return jnp.where(allowed[None], scores, -1e30)


def attend_forward(query, keys, value, segments):
    row_count = query.shape[0]
    block = min(512, row_count)
    pieces = []
    log_totals = []
    for begin in range(0, row_count, block):
        scores = masked_scores(
            query[begin : begin + block], keys, segments[begin : begin + block], segments
        )
        peak = jnp.max(scores, axis=-1, keepdims=True)
        exponent = jnp.exp(scores - peak)
        total = jnp.sum(exponent, axis=-1, keepdims=True)
        soft_low = (exponent / total).astype(jnp.bfloat16)
        pieces.append(
            jnp.einsum("hqk,khd->qhd", soft_low, value, preferred_element_type=jnp.float32)
        )
        log_totals.append(peak[..., 0] + jnp.log(total[..., 0]))
    return (jnp.concatenate(pieces, axis=0), jnp.concatenate(log_totals, axis=1))


def attend_backward(query, keys, value, segments, log_total, grad_mixed):
    row_count = query.shape[0]
    block = min(512, row_count)
    query_grads = []
    key_grad = jnp.zeros(keys.shape, jnp.float32)
    value_grad = jnp.zeros(value.shape, jnp.float32)
    for begin in range(0, row_count, block):
        query_block = query[begin : begin + block]
        grad_block = grad_mixed[begin : begin + block]
        scores = masked_scores(query_block, keys, segments[begin : begin + block], segments)
        soft = jnp.exp(scores - log_total[:, begin : begin + block, None])
        grad_soft = jnp.einsum(
            "qhd,khd->hqk", grad_block, value, preferred_element_type=jnp.float32
        )
        center = jnp.sum(soft * grad_soft, axis=-1, keepdims=True)
        grad_scores = (soft * (grad_soft - center)).astype(jnp.bfloat16)
        query_grads.append(
            jnp.einsum("hqk,khd->qhd", grad_scores, keys, preferred_element_type=jnp.float32)
            * 0.125
        )
        key_grad = (
            key_grad
            + jnp.einsum(
                "hqk,qhd->khd", grad_scores, query_block, preferred_element_type=jnp.float32
            )
            * 0.125
        )
        value_grad = value_grad + jnp.einsum(
            "hqk,qhd->khd",
            soft.astype(jnp.bfloat16),
            grad_block,
            preferred_element_type=jnp.float32,
        )
    return (jnp.concatenate(query_grads, axis=0), key_grad, value_grad)


def layer_forward(full, inputs, segments):
    (
        first_gain,
        first_shift,
        triple_weight,
        query_bias,
        value_bias,
        out_weight,
        out_bias,
        second_gain,
        second_shift,
        up_weight,
        up_bias,
        down_weight,
        down_bias,
    ) = full
    width = out_weight.shape[0]
    values = inputs.astype(jnp.float32)
    first_h, first_n, first_r = norm_forward(
        values, first_gain.astype(jnp.float32), first_shift.astype(jnp.float32)
    )
    first_in = first_h.astype(jnp.bfloat16)
    projected = jnp.dot(first_in, triple_weight, preferred_element_type=jnp.float32)
    query = (
        (projected[:, :width] + query_bias.astype(jnp.float32))
        .astype(jnp.bfloat16)
        .reshape(-1, H, HD)
    )
    keys = projected[:, width : 2 * width].astype(jnp.bfloat16).reshape(-1, H, HD)
    value = (
        (projected[:, 2 * width :] + value_bias.astype(jnp.float32))
        .astype(jnp.bfloat16)
        .reshape(-1, H, HD)
    )
    attended, log_total = attend_forward(query, keys, value, segments)
    mixed = attended.reshape(-1, width).astype(jnp.bfloat16)
    resid = (
        values
        + jnp.dot(mixed, out_weight, preferred_element_type=jnp.float32)
        + out_bias.astype(jnp.float32)
    )
    second_h, second_n, second_r = norm_forward(
        resid, second_gain.astype(jnp.float32), second_shift.astype(jnp.float32)
    )
    second_in = second_h.astype(jnp.bfloat16)
    upped = jnp.dot(second_in, up_weight, preferred_element_type=jnp.float32) + up_bias.astype(
        jnp.float32
    )
    act = jax.nn.gelu(upped, approximate=False).astype(jnp.bfloat16)
    result = (
        resid
        + jnp.dot(act, down_weight, preferred_element_type=jnp.float32)
        + down_bias.astype(jnp.float32)
    )
    saved = (
        first_n,
        first_r,
        first_in,
        query,
        keys,
        value,
        log_total,
        mixed,
        second_n,
        second_r,
        second_in,
        upped,
        act,
    )
    return (result.astype(jnp.bfloat16), saved)


def layer_backward(full, saved, grad_result, segments):
    (
        first_gain,
        first_shift,
        triple_weight,
        query_bias,
        value_bias,
        out_weight,
        out_bias,
        second_gain,
        second_shift,
        up_weight,
        up_bias,
        down_weight,
        down_bias,
    ) = full
    (
        first_n,
        first_r,
        first_in,
        query,
        keys,
        value,
        log_total,
        mixed,
        second_n,
        second_r,
        second_in,
        upped,
        act,
    ) = saved
    width = out_weight.shape[0]
    grad_out = grad_result.astype(jnp.float32)
    down_bias_part = jnp.sum(grad_out, axis=0)
    grad_low = grad_out.astype(jnp.bfloat16)
    down_weight_part = jnp.einsum("rf,rd->fd", act, grad_low, preferred_element_type=jnp.float32)
    grad_act = jnp.einsum("rd,fd->rf", grad_low, down_weight, preferred_element_type=jnp.float32)
    grad_up = grad_act * gelu_slope(upped)
    up_bias_part = jnp.sum(grad_up, axis=0)
    grad_up_low = grad_up.astype(jnp.bfloat16)
    up_weight_part = jnp.einsum(
        "rd,rf->df", second_in, grad_up_low, preferred_element_type=jnp.float32
    )
    grad_second = jnp.einsum(
        "rf,df->rd", grad_up_low, up_weight, preferred_element_type=jnp.float32
    )
    resid_part, second_gain_part, second_shift_part = norm_backward(
        grad_second, second_n, second_r, second_gain.astype(jnp.float32)
    )
    grad_resid = grad_out + resid_part
    out_bias_part = jnp.sum(grad_resid, axis=0)
    resid_low = grad_resid.astype(jnp.bfloat16)
    out_weight_part = jnp.einsum("rd,re->de", mixed, resid_low, preferred_element_type=jnp.float32)
    grad_mixed = jnp.einsum(
        "re,de->rd", resid_low, out_weight, preferred_element_type=jnp.float32
    ).astype(jnp.bfloat16)
    query_grad, key_grad, value_grad = attend_backward(
        query, keys, value, segments, log_total, grad_mixed.reshape(-1, H, HD)
    )
    query_low = query_grad.reshape(-1, width).astype(jnp.bfloat16)
    key_low = key_grad.reshape(-1, width).astype(jnp.bfloat16)
    value_low = value_grad.reshape(-1, width).astype(jnp.bfloat16)
    query_bias_part = jnp.sum(query_low, axis=0, dtype=jnp.float32)
    value_bias_part = jnp.sum(value_low, axis=0, dtype=jnp.float32)
    grad_projected = jnp.concatenate([query_low, key_low, value_low], axis=1)
    triple_weight_part = jnp.einsum(
        "rd,re->de", first_in, grad_projected, preferred_element_type=jnp.float32
    )
    grad_first = jnp.einsum(
        "re,de->rd", grad_projected, triple_weight, preferred_element_type=jnp.float32
    )
    input_part, first_gain_part, first_shift_part = norm_backward(
        grad_first, first_n, first_r, first_gain.astype(jnp.float32)
    )
    grad_inputs = (grad_resid + input_part).astype(jnp.bfloat16)
    parts = (
        first_gain_part,
        first_shift_part,
        triple_weight_part,
        query_bias_part,
        value_bias_part,
        out_weight_part,
        out_bias_part,
        second_gain_part,
        second_shift_part,
        up_weight_part,
        up_bias_part,
        down_weight_part,
        down_bias_part,
    )
    return (grad_inputs, parts)


def on_device(
    tokens,
    cotangent,
    segment_ids,
    first_gain,
    first_shift,
    triple_weight,
    query_bias,
    value_bias,
    out_weight,
    out_bias,
    second_gain,
    second_shift,
    up_weight,
    up_bias,
    down_weight,
    down_bias,
):
    shards = (
        first_gain,
        first_shift,
        triple_weight,
        query_bias,
        value_bias,
        out_weight,
        out_bias,
        second_gain,
        second_shift,
        up_weight,
        up_bias,
        down_weight,
        down_bias,
    )
    totals = tuple((jnp.zeros(piece.shape, jnp.float32) for piece in shards))
    results = []
    input_grads = []
    for micro in range(MB):
        lower = micro * ROWS
        segments = segment_ids[lower : lower + ROWS]
        forward_full = (
            lax.all_gather(first_gain, "fsdp", axis=0, tiled=True),
            lax.all_gather(first_shift, "fsdp", axis=0, tiled=True),
            lax.all_gather(triple_weight, "fsdp", axis=0, tiled=True),
            lax.all_gather(query_bias, "fsdp", axis=0, tiled=True),
            lax.all_gather(value_bias, "fsdp", axis=0, tiled=True),
            lax.all_gather(out_weight, "fsdp", axis=0, tiled=True),
            lax.all_gather(out_bias, "fsdp", axis=0, tiled=True),
            lax.all_gather(second_gain, "fsdp", axis=0, tiled=True),
            lax.all_gather(second_shift, "fsdp", axis=0, tiled=True),
            lax.all_gather(up_weight, "fsdp", axis=0, tiled=True),
            lax.all_gather(up_bias, "fsdp", axis=0, tiled=True),
            lax.all_gather(down_weight, "fsdp", axis=0, tiled=True),
            lax.all_gather(down_bias, "fsdp", axis=0, tiled=True),
        )
        result, saved = layer_forward(forward_full, tokens[lower : lower + ROWS], segments)
        results.append(result)
        backward_full = (
            lax.all_gather(first_gain, "fsdp", axis=0, tiled=True),
            lax.all_gather(first_shift, "fsdp", axis=0, tiled=True),
            lax.all_gather(triple_weight, "fsdp", axis=0, tiled=True),
            lax.all_gather(query_bias, "fsdp", axis=0, tiled=True),
            lax.all_gather(value_bias, "fsdp", axis=0, tiled=True),
            lax.all_gather(out_weight, "fsdp", axis=0, tiled=True),
            lax.all_gather(out_bias, "fsdp", axis=0, tiled=True),
            lax.all_gather(second_gain, "fsdp", axis=0, tiled=True),
            lax.all_gather(second_shift, "fsdp", axis=0, tiled=True),
            lax.all_gather(up_weight, "fsdp", axis=0, tiled=True),
            lax.all_gather(up_bias, "fsdp", axis=0, tiled=True),
            lax.all_gather(down_weight, "fsdp", axis=0, tiled=True),
            lax.all_gather(down_bias, "fsdp", axis=0, tiled=True),
        )
        grad_inputs, parts = layer_backward(
            backward_full, saved, cotangent[lower : lower + ROWS], segments
        )
        input_grads.append(grad_inputs)
        p0, p1, p2, p3, p4, p5, p6, p7, p8, p9, p10, p11, p12 = parts
        summed = (
            lax.psum_scatter(p0, "fsdp", scatter_dimension=0, tiled=True),
            lax.psum_scatter(p1, "fsdp", scatter_dimension=0, tiled=True),
            lax.psum_scatter(p2, "fsdp", scatter_dimension=0, tiled=True),
            lax.psum_scatter(p3, "fsdp", scatter_dimension=0, tiled=True),
            lax.psum_scatter(p4, "fsdp", scatter_dimension=0, tiled=True),
            lax.psum_scatter(p5, "fsdp", scatter_dimension=0, tiled=True),
            lax.psum_scatter(p6, "fsdp", scatter_dimension=0, tiled=True),
            lax.psum_scatter(p7, "fsdp", scatter_dimension=0, tiled=True),
            lax.psum_scatter(p8, "fsdp", scatter_dimension=0, tiled=True),
            lax.psum_scatter(p9, "fsdp", scatter_dimension=0, tiled=True),
            lax.psum_scatter(p10, "fsdp", scatter_dimension=0, tiled=True),
            lax.psum_scatter(p11, "fsdp", scatter_dimension=0, tiled=True),
            lax.psum_scatter(p12, "fsdp", scatter_dimension=0, tiled=True),
        )
        totals = tuple((left + right for left, right in zip(totals, summed)))
    s0, s1, s2, s3, s4, s5, s6, s7, s8, s9, s10, s11, s12 = totals
    final = (
        lax.psum(s0.astype(jnp.bfloat16), "dp").astype(jnp.float32),
        lax.psum(s1.astype(jnp.bfloat16), "dp").astype(jnp.float32),
        lax.psum(s2.astype(jnp.bfloat16), "dp").astype(jnp.float32),
        lax.psum(s3.astype(jnp.bfloat16), "dp").astype(jnp.float32),
        lax.psum(s4.astype(jnp.bfloat16), "dp").astype(jnp.float32),
        lax.psum(s5.astype(jnp.bfloat16), "dp").astype(jnp.float32),
        lax.psum(s6.astype(jnp.bfloat16), "dp").astype(jnp.float32),
        lax.psum(s7.astype(jnp.bfloat16), "dp").astype(jnp.float32),
        lax.psum(s8.astype(jnp.bfloat16), "dp").astype(jnp.float32),
        lax.psum(s9.astype(jnp.bfloat16), "dp").astype(jnp.float32),
        lax.psum(s10.astype(jnp.bfloat16), "dp").astype(jnp.float32),
        lax.psum(s11.astype(jnp.bfloat16), "dp").astype(jnp.float32),
        lax.psum(s12.astype(jnp.bfloat16), "dp").astype(jnp.float32),
    )
    return (
        jnp.concatenate(results, axis=0),
        jnp.concatenate(input_grads, axis=0),
        final[0],
        final[1],
        final[2],
        final[3],
        final[4],
        final[5],
        final[6],
        final[7],
        final[8],
        final[9],
        final[10],
        final[11],
        final[12],
    )


def solution(mesh):
    in_specs = (
        P(("dp", "fsdp"), None),
        P(("dp", "fsdp"), None),
        P(("dp", "fsdp")),
        P("fsdp"),
        P("fsdp"),
        P("fsdp", None),
        P("fsdp"),
        P("fsdp"),
        P("fsdp", None),
        P("fsdp"),
        P("fsdp"),
        P("fsdp"),
        P("fsdp", None),
        P("fsdp"),
        P("fsdp", None),
        P("fsdp"),
    )
    out_specs = (
        P(("dp", "fsdp"), None),
        P(("dp", "fsdp"), None),
        P("fsdp"),
        P("fsdp"),
        P("fsdp", None),
        P("fsdp"),
        P("fsdp"),
        P("fsdp", None),
        P("fsdp"),
        P("fsdp"),
        P("fsdp"),
        P("fsdp", None),
        P("fsdp"),
        P("fsdp", None),
        P("fsdp"),
    )
    return jax.shard_map(
        on_device, mesh=mesh, in_specs=in_specs, out_specs=out_specs, check_vma=False
    )
```

profile of v0, /device:TPU:0, one launch (start us, length us, event | category | flops | bytes accessed | tf_op | source)
XLA Modules:
  0.0 1104.1 jit_solution(5142248432136446658)
XLA Ops:
  21.7 63.5 %all-reduce.19 = (bf16[768]{0:T(1024)(128)(2,1)S(1)}, bf16[768]{0:T(1024)(128)(2,1)S(1)}, bf16[768]{0:T(1024)(128)(2,1)S(1)}, bf16[768]{0:T(1024)(128)(2,1)S(1)}...) all-reduce(bf16[768]{0:T(1024)(128)(2,1)S(1)} %dynamic-update-slice, ...), channel_id=1, replica_groups=mesh['dp'=2,'fsdp'=16] {'fsdp'}, use_global_device_ids=true, to_apply=%add.1 | all-reduce | flops 9216 | bytes 36864
  144.8 12.3 %fusion.55 = (f32[12,512]{1,0:T(8,128)S(1)}, f32[12,512,1024]{2,1,0:T(8,128)}) fusion(pred[512,1024]{1,0:T(8,128)(4,1)} %get-tuple-element.151, bf16[512,12,64]{0,2,1:T(8,128)(2,1)} %bitcast.134, bf16[1024,12,64]{0,2,1:T(8,128)(2,1)S(1)} %bitcast.116), kind=kOutput, calls=%fused_computation.95 | convolution fusion | flops 824174592 | bytes 28073984 | tf_op jit(solution)/shard_map/qhd,khd->hqk/dot_general | solution.py:40
  157.1 12.5 %fusion.1 = f32[12,512]{1,0:T(8,128)S(1)} fusion(f32[12,512]{1,0:T(8,128)S(1)} %get-tuple-element.122, f32[12,512,1024]{2,1,0:T(8,128)} %get-tuple-element.123, pred[512,1024]{1,0:T(8,128)(4,1)} %get-tuple-element.151), kind=kLoop, calls=%fused_computation.25 | loop fusion | flops 25159680 | bytes 25739264 | tf_op jit(solution)/shard_map/reduce_sum | solution.py:57
  182.8 12.1 %fusion.54 = (f32[12,512]{1,0:T(8,128)S(1)}, f32[12,512,1024]{2,1,0:T(8,128)}) fusion(pred[512,1024]{1,0:T(8,128)(4,1)} %get-tuple-element.152, bf16[512,12,64]{0,2,1:T(8,128)(2,1)} %bitcast.136, bf16[1024,12,64]{0,2,1:T(8,128)(2,1)S(1)} %bitcast.117), kind=kOutput, calls=%fused_computation.94 | convolution fusion | flops 824174592 | bytes 28073984 | tf_op jit(solution)/shard_map/qhd,khd->hqk/dot_general | solution.py:40
  194.9 13.6 %fusion = f32[12,512]{1,0:T(8,128)S(1)} fusion(f32[12,512]{1,0:T(8,128)S(1)} %get-tuple-element.124, f32[12,512,1024]{2,1,0:T(8,128)} %get-tuple-element.125, pred[512,1024]{1,0:T(8,128)(4,1)} %get-tuple-element.152), kind=kLoop, calls=%fused_computation.24 | loop fusion | flops 25159680 | bytes 25739264 | tf_op jit(solution)/shard_map/reduce_sum | solution.py:57
  219.8 12.3 %fusion.57 = (f32[12,512]{1,0:T(8,128)S(1)}, f32[12,512,1024]{2,1,0:T(8,128)}) fusion(pred[512,1024]{1,0:T(8,128)(4,1)S(1)} %copy-done.29, bf16[512,12,64]{0,2,1:T(8,128)(2,1)} %bitcast.132, bf16[1024,12,64]{0,2,1:T(8,128)(2,1)S(1)} %bitcast.120), kind=kOutput, calls=%fused_computation.97 | convolution fusion | flops 824174592 | bytes 28073984 | tf_op jit(solution)/shard_map/qhd,khd->hqk/dot_general | solution.py:40
  232.1 12.3 %fusion.3 = f32[12,512]{1,0:T(8,128)S(1)} fusion(f32[12,512]{1,0:T(8,128)S(1)} %get-tuple-element.118, f32[12,512,1024]{2,1,0:T(8,128)} %get-tuple-element.119, pred[512,1024]{1,0:T(8,128)(4,1)S(1)} %copy-done.29), kind=kLoop, calls=%fused_computation.27 | loop fusion | flops 25159680 | bytes 25739264 | tf_op jit(solution)/shard_map/reduce_sum | solution.py:57
  255.9 12.0 %fusion.56 = (f32[12,512]{1,0:T(8,128)S(1)}, f32[12,512,1024]{2,1,0:T(8,128)}) fusion(pred[512,1024]{1,0:T(8,128)(4,1)S(1)} %copy-done.26, bf16[512,12,64]{0,2,1:T(8,128)(2,1)} %bitcast.138, bf16[1024,12,64]{0,2,1:T(8,128)(2,1)S(1)} %bitcast.121), kind=kOutput, calls=%fused_computation.96 | convolution fusion | flops 824174592 | bytes 28073984 | tf_op jit(solution)/shard_map/qhd,khd->hqk/dot_general | solution.py:40
  268.0 12.3 %fusion.2 = f32[12,512]{1,0:T(8,128)S(1)} fusion(f32[12,512]{1,0:T(8,128)S(1)} %get-tuple-element.120, f32[12,512,1024]{2,1,0:T(8,128)} %get-tuple-element.121, pred[512,1024]{1,0:T(8,128)(4,1)S(1)} %copy-done.26), kind=kLoop, calls=%fused_computation.26 | loop fusion | flops 25159680 | bytes 25739264 | tf_op jit(solution)/shard_map/reduce_sum | solution.py:57
  304.6 11.0 fusion.153
  315.6 13.5 %fusion.166 = (f32[3072]{0:T(1024)}, bf16[1024,3072]{1,0:T(8,128)(2,1)S(1)}) fusion(f32[1024,3072]{1,0:T(8,128)} %fusion.153, f32[3072]{0:T(1024)S(1)} %copy-done.99, bf16[3072,768]{1,0:T(8,128)(2,1)} %all-gather.11.cloned.1.call-done, bf16[2048,768]{1,0:T(8,128)(2,1)} %param.17), kind=kOutput, calls=%fused_computation.289 | convolution fusion | flops 4869583872 | bytes 25190400 | tf_op jit(solution)/shard_map/rd,fd->rf/dot_general | solution.py:210
  335.8 61.5 %fusion.10 = (bf16[1024,3072]{1,0:T(8,128)(2,1)}, bf16[1024,3072]{1,0:T(8,128)(2,1)}, f32[1024,3072]{1,0:T(8,128)}) fusion(f32[3072]{0:T(1024)S(1)} %copy-done.99, f32[1024,3072]{1,0:T(8,128)S(1)} %bitcast.165, bf16[768,3072]{1,0:T(8,128)(2,1)S(1)} %copy-done.110, f32[1024,768]{1,0:T(8,128)S(1)} %get-tuple-element.127, f32[768]{0:T(1024)S(1)} %copy-done.64, ...), kind=kOutput, calls=%fused_computation.38 | convolution fusion | flops 5251006464 | bytes 45639680 | tf_op jit(solution)/shard_map/dot_general | solution.py:147
  397.4 12.0 %fusion.165 = (f32[3072]{0:T(1024)}, bf16[1024,3072]{1,0:T(8,128)(2,1)S(1)}) fusion(f32[1024,3072]{1,0:T(8,128)} %get-tuple-element.130, f32[3072]{0:T(1024)S(1)} %copy-done.99, bf16[3072,768]{1,0:T(8,128)(2,1)} %all-gather.11.cloned.1.call-done, bf16[2048,768]{1,0:T(8,128)(2,1)S(1)} %copy-done.48), kind=kOutput, calls=%fused_computation.288 | convolution fusion | flops 4869583872 | bytes 25190400 | tf_op jit(solution)/shard_map/rd,fd->rf/dot_general | solution.py:210
  409.4 12.9 %multiply_reduce_fusion.5 = (f32[768]{0:T(1024)}, f32[1024]{0:T(1024)S(1)}, f32[1024]{0:T(1024)S(1)}, f32[768]{0:T(1024)}, f32[768]{0:T(1024)}, /*index=5*/f32[1...) fusion(f32[1024,768]{1,0:T(8,128)S(1)} %get-tuple-element.127, f32[1024]{0:T(1024)S(1)} %add_rsqrt_fusion.2, ...), kind=kOutput, calls=%fused_computation.160 | convolution fusion | flops 4845985792 | bytes 23641088 | tf_op jit(solution)/shard_map/rf,df->rd/dot_general | solution.py:217
  431.6 21.7 %multiply_reduce_fusion.1 = (f32[12,512]{1,0:T(8,128)S(1)}, f32[12,512,1024]{2,1,0:T(8,128)}) fusion(f32[12,512]{1,0:T(8,128)S(1)} %copy-done.71, f32[12,512,1024]{2,1,0:T(8,128)} %get-tuple-element.121, pred[512,1024]{1,0:T(8,128)(4,1)S(1)} %copy-done.27, bf16[512,12,64]{0,2,1:T(8,128)(2,1)S(1)} %bitcast.146, bf16[1024,12,64]{0,2,1:T(8,128)(2,1)S(1)} %bitcast.130), kind=kOutput, calls=%fused_computation.4 | convolution fusion | flops 836757504 | bytes 53264384 | tf_op jit(solution)/shard_map/qhd,khd->hqk/dot_general | solution.py:77
  453.3 17.4 %multiply_convert_fusion.1 = bf16[12,512,1024]{2,1,0:T(8,128)(2,1)S(1)} fusion(f32[12,512,1024]{2,1,0:T(8,128)} %get-tuple-element.137, f32[12,512]{1,0:T(8,128)S(1)} %get-tuple-element.136, f32[12,512]{1,0:T(8,128)S(1)} %copy-done.71, f32[12,512,1024]{2,1,0:T(8,128)} %get-tuple-element.121, pred[512,1024]{1,0:T(8,128)(4,1)} %get-tuple-element.114), kind=kLoop, calls=%fused_computation.3 | loop fusion | flops 37748736 | bytes 63488000 | tf_op jit(solution)/shard_map/convert_element_type | solution.py:81
  482.2 13.2 %fusion.24 = f32[12,64,1024]{2,1,0:T(8,128)} fusion(bf16[512,12,64]{0,2,1:T(8,128)(2,1)S(1)} %bitcast.150, f32[12,512]{1,0:T(8,128)S(1)} %copy-done.74, f32[12,512,1024]{2,1,0:T(8,128)} %get-tuple-element.119, pred[512,1024]{1,0:T(8,128)(4,1)S(1)} %copy-done.30), kind=kOutput, calls=%fused_computation.52 | convolution fusion | flops 830472192 | bytes 29646848 | tf_op jit(solution)/shard_map/hqk,qhd->khd/dot_general | solution.py:93
  495.4 21.8 %multiply_reduce_fusion = (f32[12,512]{1,0:T(8,128)S(1)}, f32[12,512,1024]{2,1,0:T(8,128)}) fusion(f32[12,512]{1,0:T(8,128)S(1)} %copy-done.74, f32[12,512,1024]{2,1,0:T(8,128)} %get-tuple-element.119, pred[512,1024]{1,0:T(8,128)(4,1)S(1)} %copy-done.31, bf16[512,12,64]{0,2,1:T(8,128)(2,1)S(1)} %bitcast.151, bf16[1024,12,64]{0,2,1:T(8,128)(2,1)S(1)} %bitcast.131), kind=kOutput, calls=%fused_computation.1 | convolution fusion | flops 836757504 | bytes 53264384 | tf_op jit(solution)/shard_map/qhd,khd->hqk/dot_general | solution.py:77
  525.0 21.6 %multiply_reduce_fusion.3 = (f32[12,512]{1,0:T(8,128)S(1)}, f32[12,512,1024]{2,1,0:T(8,128)}) fusion(f32[12,512]{1,0:T(8,128)S(1)} %copy-done.75, f32[12,512,1024]{2,1,0:T(8,128)} %get-tuple-element.125, pred[512,1024]{1,0:T(8,128)(4,1)S(1)} %copy-done.33, bf16[512,12,64]{0,2,1:T(8,128)(2,1)S(1)} %bitcast.148, bf16[1024,12,64]{0,2,1:T(8,128)(2,1)S(1)} %bitcast.127), kind=kOutput, calls=%fused_computation.10 | convolution fusion | flops 836757504 | bytes 53264384 | tf_op jit(solution)/shard_map/qhd,khd->hqk/dot_general | solution.py:77
  546.6 17.2 %multiply_convert_fusion.3 = bf16[12,512,1024]{2,1,0:T(8,128)(2,1)S(1)} fusion(f32[12,512,1024]{2,1,0:T(8,128)} %get-tuple-element.133, f32[12,512]{1,0:T(8,128)S(1)} %get-tuple-element.132, f32[12,512]{1,0:T(8,128)S(1)} %copy-done.75, f32[12,512,1024]{2,1,0:T(8,128)} %get-tuple-element.125, pred[512,1024]{1,0:T(8,128)(4,1)} %get-tuple-element.152), kind=kLoop, calls=%fused_computation.9 | loop fusion | flops 37748736 | bytes 63488000 | tf_op jit(solution)/shard_map/convert_element_type | solution.py:81
  575.3 13.3 %fusion.28 = f32[12,64,1024]{2,1,0:T(8,128)} fusion(bf16[512,12,64]{0,2,1:T(8,128)(2,1)S(1)} %bitcast.153, f32[12,512]{1,0:T(8,128)S(1)} %copy-done.73, f32[12,512,1024]{2,1,0:T(8,128)} %get-tuple-element.123, pred[512,1024]{1,0:T(8,128)(4,1)S(1)} %copy-done.28), kind=kOutput, calls=%fused_computation.54 | convolution fusion | flops 830472192 | bytes 29646848 | tf_op jit(solution)/shard_map/hqk,qhd->khd/dot_general | solution.py:93
  588.5 18.4 %multiply_reduce_fusion.2 = (f32[12,512]{1,0:T(8,128)S(1)}, f32[12,512,1024]{2,1,0:T(8,128)}) fusion(f32[12,512]{1,0:T(8,128)S(1)} %copy-done.73, f32[12,512,1024]{2,1,0:T(8,128)} %get-tuple-element.123, pred[512,1024]{1,0:T(8,128)(4,1)} %get-tuple-element.151, bf16[512,12,64]{0,2,1:T(8,128)(2,1)} %bitcast.152, bf16[1024,12,64]{0,2,1:T(8,128)(2,1)} %bitcast.124), kind=kOutput, calls=%fused_computation.7 | convolution fusion | flops 836757504 | bytes 53264384 | tf_op jit(solution)/shard_map/qhd,khd->hqk/dot_general | solution.py:77
  611.9 15.1 %convert_reduce_fusion.5 = (f32[12,64]{1,0:T(8,128)S(1)}, bf16[12,64,1024]{2,1,0:T(8,128)(2,1)}) fusion(f32[12,64,1024]{2,1,0:T(8,128)} %fusion.28, bf16[512,12,64]{0,2,1:T(8,128)(2,1)} %bitcast.149, f32[12,512]{1,0:T(8,128)S(1)} %copy-done.75, f32[12,512,1024]{2,1,0:T(8,128)} %get-tuple-element.125, pred[512,1024]{1,0:T(8,128)(4,1)} %get-tuple-element.152), kind=kOutput, calls=%fused_computation.162 | convolution fusion | flops 833617152 | bytes 31222784 | tf_op jit(solution)/shard_map/hqk,qhd->khd/dot_general | solution.py:93
  627.0 17.6 %multiply_convert_fusion = bf16[12,512,1024]{2,1,0:T(8,128)(2,1)S(1)} fusion(f32[12,512,1024]{2,1,0:T(8,128)} %get-tuple-element.139, f32[12,512]{1,0:T(8,128)S(1)} %get-tuple-element.138, f32[12,512]{1,0:T(8,128)S(1)} %copy-done.74, f32[12,512,1024]{2,1,0:T(8,128)} %get-tuple-element.119, pred[512,1024]{1,0:T(8,128)(4,1)} %get-tuple-element.115), kind=kLoop, calls=%fused_computation | loop fusion | flops 37748736 | bytes 63488000 | tf_op jit(solution)/shard_map/convert_element_type | solution.py:81
  650.9 22.7 %multiply_convert_fusion.2 = bf16[12,512,1024]{2,1,0:T(8,128)(2,1)} fusion(f32[12,512,1024]{2,1,0:T(8,128)} %get-tuple-element.135, f32[12,512]{1,0:T(8,128)S(1)} %get-tuple-element.134, f32[12,512]{1,0:T(8,128)S(1)} %copy-done.73, f32[12,512,1024]{2,1,0:T(8,128)} %get-tuple-element.123, pred[512,1024]{1,0:T(8,128)(4,1)} %get-tuple-element.151), kind=kLoop, calls=%fused_computation.6 | loop fusion | flops 37748736 | bytes 63488000 | tf_op jit(solution)/shard_map/convert_element_type | solution.py:81
  706.5 13.3 %convert_reduce_fusion.4 = (f32[12,64]{1,0:T(8,128)S(1)}, bf16[12,64,1024]{2,1,0:T(8,128)(2,1)S(1)}) fusion(f32[12,64,1024]{2,1,0:T(8,128)} %fusion.24, bf16[512,12,64]{0,2,1:T(8,128)(2,1)} %bitcast.147, f32[12,512]{1,0:T(8,128)S(1)} %copy-done.72, f32[12,512,1024]{2,1,0:T(8,128)} %get-tuple-element.121, pred[512,1024]{1,0:T(8,128)(4,1)} %get-tuple-element.114), kind=kOutput, calls=%fused_computation.161 | convolution fusion | flops 833617152 | bytes 31222784 | tf_op jit(solution)/shard_map/hqk,qhd->khd/dot_general | solution.py:93
  741.8 11.6 %convolution_add_fusion.2 = f32[768,3072]{1,0:T(8,128)} fusion(f32[768,3072]{1,0:T(8,128)S(1)} %fusion.97, bf16[1024,3072]{1,0:T(8,128)(2,1)} %copy-done.40, f32[1024,768]{1,0:T(8,128)S(1)} %copy-done.16, f32[1024]{0:T(1024)S(1)} %copy-done.82, f32[1024]{0:T(1024)S(1)} %copy-done.70, f32[768]{0:T(1024)S(1)} %copy-done.65, f32[768]{0:T(1024)S(1)} %copy-done.63), kind=kOutput, calls=%fused_computation.100 | convolution fusion | flops 4838129664 | bytes 28325888 | tf_op jit(solution)/shard_map/rd,rf->df/dot_general | solution.py:214
  761.4 10.5 convolution_add_fusion.1
  789.2 58.9 %all-reduce.18 = (bf16[768]{0:T(1024)(128)(2,1)S(1)}, bf16[768]{0:T(1024)(128)(2,1)S(1)}, bf16[768]{0:T(1024)(128)(2,1)S(1)}, bf16[768]{0:T(1024)(128)(2,1)S(1)}...) all-reduce(f32[768]{0:T(1024)S(1)} %add.387, ...), channel_id=15, replica_groups=mesh['dp'=2,'fsdp'=16] {'fsdp'}, use_global_device_ids=true, to_apply=%region_29.30.clone | all-reduce | flops 9216 | bytes 55296
  881.2 52.8 %reduce-scatter.9.cloned.1.call-done = f32[48,3072]{1,0:T(8,128)} async-done(((f32[768,3072]{1,0:T(8,128)}), f32[48,3072]{1,0:T(8,128)}) %reduce-scatter.9.cloned.1.call-update) | async-done | bytes 589840 | tf_op jit(solution)/shard_map/reduce_scatter | solution.py:353
  935.7 114.0 %reduce-scatter.11.cloned.1.call-done = f32[192,768]{1,0:T(8,128)} async-done(((f32[3072,768]{1,0:T(8,128)}), f32[192,768]{1,0:T(8,128)}) %reduce-scatter.11.cloned.1.call-update) | async-done | bytes 589840 | tf_op jit(solution)/shard_map/reduce_scatter | solution.py:355
  1059.4 30.7 %all-reduce.24.cloned.1.call-done = (bf16[48,2304]{1,0:T(8,128)(2,1)}, bf16[48,768]{1,0:T(8,128)(2,1)}, bf16[48,3072]{1,0:T(8,128)(2,1)}, bf16[192,768]{1,0:T(8,128)(2,1)}) async-done(((bf16[48,2304]{1,0:T(8,128)(2,1)}, bf16[48,768]{1,0:T(8,128)(2,1)}, bf16[48,3072]{1,0:T(8,128)(2,1)}, bf16[192,768]{1,0:T(8,128)(2,1)}), (bf16[48,2304]{1,0:T(8,128)(2,1)}, bf16[48,768]{1,0:T(8,128)(2,1)}, ...) | async-done | bytes 884752 | tf_op jit(solution)/shard_map/psum | solution.py:363
  (411 shorter events, 320.1 us)
Async XLA Ops:
  7.2 82.3 %copy-start.8 = (bf16[2048,768]{1,0:T(8,128)(2,1)S(1)}, bf16[2048,768]{1,0:T(8,128)(2,1)}, u32[]{:S(2)}) copy-start(bf16[2048,768]{1,0:T(8,128)(2,1)} %param.16) | copy-start | bytes 9437188
  7.2 86.4 %all-gather.5.cloned.1.call-start = ((), (), s32[]{:S(2)}) async-start(), calls=%async_computation.4 | async-start | bytes 3760128 | tf_op jit(solution)/shard_map/all_gather | solution.py:309
  7.9 285.6 %all-gather.7.cloned.1.call-start = ((), (), s32[]{:S(2)}) async-start(), calls=%async_computation.5 | async-start | bytes 1253376 | tf_op jit(solution)/shard_map/all_gather | solution.py:312
  8.7 295.9 %all-gather.9.cloned.1.call-start = ((), (), s32[]{:S(2)}) async-start(), calls=%async_computation.6 | async-start | bytes 5013504 | tf_op jit(solution)/shard_map/all_gather | solution.py:316
  9.4 306.1 %all-gather.11.cloned.1.call-start = ((), (), s32[]{:S(2)}) async-start(), calls=%async_computation.7 | async-start | bytes 5013504 | tf_op jit(solution)/shard_map/all_gather | solution.py:318
  10.0 867.7 %reduce-scatter.7.cloned.1.call-start = ((), (), s32[]{:S(2)}) async-start(), calls=%async_computation.9 | async-start | bytes 2506752 | tf_op jit(solution)/shard_map/reduce_scatter | solution.py:349
  85.2 19.1 %copy-start.106 = (f32[768]{0:T(1024)}, f32[768]{0:T(1024)S(1)}, u32[]{:S(2)}) copy-start(f32[768]{0:T(1024)S(1)} %convert_element_type.312) | copy-start | bytes 9220
  85.2 19.1 %copy-start.93 = (f32[768]{0:T(1024)}, f32[768]{0:T(1024)S(1)}, u32[]{:S(2)}) copy-start(f32[768]{0:T(1024)S(1)} %convert_element_type.311) | copy-start | bytes 9220
  104.3 151.6 %copy-start.5 = (bf16[1024,768]{0,1:T(8,128)(2,1)}, bf16[1024,768]{0,1:T(8,128)(2,1)S(1)}, u32[]{:S(2)}) copy-start(bf16[1024,768]{0,1:T(8,128)(2,1)S(1)} %copy.69) | copy-start | bytes 4718596
  118.2 64.6 %copy-start.4 = (bf16[1024,768]{0,1:T(8,128)(2,1)}, bf16[1024,768]{0,1:T(8,128)(2,1)S(1)}, u32[]{:S(2)}) copy-start(bf16[1024,768]{0,1:T(8,128)(2,1)S(1)} %copy.65) | copy-start | bytes 4718596
  144.8 24.9 %copy-start.21 = (bf16[1024,768]{0,1:T(8,128)(2,1)S(1)}, bf16[1024,768]{0,1:T(8,128)(2,1)}, u32[]{:S(2)}) copy-start(bf16[1024,768]{0,1:T(8,128)(2,1)} %copy.63) | copy-start | bytes 4718596
  157.1 16.2 %copy-start.1 = (f32[12,512,1024]{2,1,0:T(8,128)S(1)}, f32[12,512,1024]{2,1,0:T(8,128)}, u32[]{:S(2)}) copy-start(f32[12,512,1024]{2,1,0:T(8,128)} %get-tuple-element.123) | copy-start | bytes 75497472
  194.9 16.3 %copy-start.3 = (f32[12,512,1024]{2,1,0:T(8,128)S(1)}, f32[12,512,1024]{2,1,0:T(8,128)}, u32[]{:S(2)}) copy-start(f32[12,512,1024]{2,1,0:T(8,128)} %get-tuple-element.125) | copy-start | bytes 75497472
  194.9 16.4 %copy-start.32 = (pred[512,1024]{1,0:T(8,128)(4,1)S(1)}, pred[512,1024]{1,0:T(8,128)(4,1)}, u32[]{:S(2)}) copy-start(pred[512,1024]{1,0:T(8,128)(4,1)} %get-tuple-element.152) | copy-start | bytes 1572868
  219.7 24.6 %copy-start.23 = (bf16[1024,768]{0,1:T(8,128)(2,1)S(1)}, bf16[1024,768]{0,1:T(8,128)(2,1)}, u32[]{:S(2)}) copy-start(bf16[1024,768]{0,1:T(8,128)(2,1)} %copy.67) | copy-start | bytes 4718596
  255.9 24.4 %copy-start.60 = (bf16[512,12,64]{0,2,1:T(8,128)(2,1)S(1)}, bf16[512,12,64]{0,2,1:T(8,128)(2,1)}, u32[]{:S(2)}) copy-start(bf16[512,12,64]{0,2,1:T(8,128)(2,1)} %fusion.113) | copy-start | bytes 2359300
  268.0 16.1 %copy-start = (f32[12,512,1024]{2,1,0:T(8,128)S(1)}, f32[12,512,1024]{2,1,0:T(8,128)}, u32[]{:S(2)}) copy-start(f32[12,512,1024]{2,1,0:T(8,128)} %get-tuple-element.121) | copy-start | bytes 75497472
  297.5 124.8 %copy-start.6 = (f32[1024,768]{1,0:T(8,128)}, f32[1024,768]{1,0:T(8,128)S(1)}, u32[]{:S(2)}) copy-start(f32[1024,768]{1,0:T(8,128)S(1)} %get-tuple-element.127) | copy-start | bytes 9437188
  297.6 124.8 %copy-start.66 = (f32[1024]{0:T(1024)}, f32[1024]{0:T(1024)S(1)}, u32[]{:S(2)}) copy-start(f32[1024]{0:T(1024)S(1)} %broadcast_multiply_fusion.10) | copy-start | bytes 12292
  298.1 124.3 %copy-start.78 = (f32[1024]{0:T(1024)}, f32[1024]{0:T(1024)S(1)}, u32[]{:S(2)}) copy-start(f32[1024]{0:T(1024)S(1)} %add_rsqrt_fusion.2) | copy-start | bytes 12292
  299.8 15.7 %copy-start.68 = (f32[1024]{0:T(1024)}, f32[1024]{0:T(1024)S(1)}, u32[]{:S(2)}) copy-start(f32[1024]{0:T(1024)S(1)} %broadcast_multiply_fusion.8) | copy-start | bytes 12292
  315.6 20.2 %slice-start = ((s8[12582912]{0:T(1024)(128)(4,1)}), s8[4194304]{0:T(1024)(128)(4,1)S(1)}, s32[]{:S(2)}) async-start(s8[12582912]{0:T(1024)(128)(4,1)} %bitcast.164), calls=%async_computation.13 | async-start | bytes 8388608
  315.6 20.2 %slice-start.1 = ((s8[12582912]{0:T(1024)(128)(4,1)}), s8[4194304]{0:T(1024)(128)(4,1)S(1)}, s32[]{:S(2)}) async-start(s8[12582912]{0:T(1024)(128)(4,1)} %bitcast.164), calls=%async_computation.14 | async-start | bytes 8388608
  335.8 61.6 %copy-start.48 = (bf16[2048,768]{1,0:T(8,128)(2,1)S(1)}, bf16[2048,768]{1,0:T(8,128)(2,1)}, u32[]{:S(2)}) copy-start(bf16[2048,768]{1,0:T(8,128)(2,1)} %param.17) | copy-start | bytes 9437188
  431.6 21.7 %copy-start.52 = (bf16[512,768]{0,1:T(8,128)(2,1)}, bf16[512,768]{0,1:T(8,128)(2,1)S(1)}, u32[]{:S(2)}) copy-start(bf16[512,768]{0,1:T(8,128)(2,1)S(1)} %get-tuple-element.92) | copy-start | bytes 2359300
  525.0 21.6 %copy-start.53 = (bf16[512,768]{0,1:T(8,128)(2,1)}, bf16[512,768]{0,1:T(8,128)(2,1)S(1)}, u32[]{:S(2)}) copy-start(bf16[512,768]{0,1:T(8,128)(2,1)S(1)} %get-tuple-element.90) | copy-start | bytes 2359300
  588.5 18.4 %copy-start.19 = (f32[1024,768]{1,0:T(8,128)S(1)}, f32[1024,768]{1,0:T(8,128)}, u32[]{:S(2)}) copy-start(f32[1024,768]{1,0:T(8,128)} %copy-done.18) | copy-start | bytes 9437188
  611.9 267.6 %reduce-scatter.5.cloned.1.call-start = ((), (), s32[]{:S(2)}) async-start(), calls=%async_computation.8 | async-start | bytes 7520256 | tf_op jit(solution)/shard_map/reduce_scatter | solution.py:346
  731.3 202.6 %reduce-scatter.9.cloned.1.call-start = ((), (), s32[]{:S(2)}) async-start(), calls=%async_computation.10 | async-start | bytes 10027008 | tf_op jit(solution)/shard_map/reduce_scatter | solution.py:353
  753.5 296.2 %reduce-scatter.11.cloned.1.call-start = ((), (), s32[]{:S(2)}) async-start(), calls=%async_computation.11 | async-start | bytes 10027008 | tf_op jit(solution)/shard_map/reduce_scatter | solution.py:355
  772.1 318.1 %all-reduce.24.cloned.1.call-start = ((), (), s32[]{:S(2)}) async-start(), calls=%async_computation.12 | async-start | bytes 1769472 | tf_op jit(solution)/shard_map/psum | solution.py:363
  875.8 175.8 %copy-start.13 = (bf16[2048,768]{1,0:T(8,128)(2,1)S(1)}, bf16[2048,768]{1,0:T(8,128)(2,1)}, u32[]{:S(2)}) copy-start(bf16[2048,768]{1,0:T(8,128)(2,1)} %param.16) | copy-start | bytes 9437188
  (98 other events, 672.5 us)
Sparse Core Ops, SparseCore 0:
  10.3 49.9 all-gather.4
  62.6 37.2 all-gather.6
  102.2 52.1 all-gather.8
  156.5 51.7 all-gather.10
  612.0 60.1 reduce-scatter.6
  731.4 87.4 reduce-scatter.4
  823.0 110.8 reduce-scatter.8
  938.6 111.0 reduce-scatter.10
  1053.3 36.7 all-reduce.23
where the time goes:
time: 1120 us; the launch traced here: 1100 us
  matrix products  511 us (46%)
  waiting for transfers between devices  200 us (18%)
  other arithmetic  186 us (17%)
  blocking collectives  127 us (11%)
  local copies, waits for them, and re-layouts  60.9 us (5%)
  between operations  18.3 us (2%)
    unnamed x2, blocking collectives  122 us
    reduce_scatter x1, waiting for transfers between devices, on_device(): lax.psum_scatter(p11, 'fsdp', scatter_dimension=0, tiled=True)  114 us
    dot_general x4, matrix products, attend_backward(): jnp.einsum('qhd,khd->hqk', grad_block, value, preferred_element_type=jnp....  83.5 us
    convert_element_type x4, other arithmetic, attend_backward(): grad_scores = (soft * (grad_soft - center)).astype(jnp.bfloat16)  74.9 us
    dot_general x2, matrix products, layer_forward(): jnp.dot(second_in, up_weight, preferred_element_type=jnp.float32)  72.5 us
    dot_general x4, matrix products, attend_backward(): jnp.einsum('hqk,qhd->khd', soft.astype(jnp.bfloat16), grad_block, preferr...  54.9 us
    reduce_scatter x1, waiting for transfers between devices, on_device(): lax.psum_scatter(p9, 'fsdp', scatter_dimension=0, tiled=True)  52.8 us
    reduce_sum x4, other arithmetic, attend_forward(): total = jnp.sum(exponent, axis=-1, keepdims=True)  50.7 us
  transfers between devices with their start and end apart: 9, of which 3 were waited for; matrix products, arithmetic and copies ran while one was open for 39% of the time, Pallas kernels for 0%

commit v1 on v0

--- a/solution.py
+++ b/solution.py
@@ -10,6 +10,11 @@
 norm_eps = 1e-06
 root_half = 0.7071067811865476
 root_inv_two_pi = 0.3989422804014327
+
+
+def _keep_up_gates(block_here, named_axis):
+    b_next = jnp.sum(lax.all_gather(block_here, named_axis), 0)
+    return b_next
 
 
 def norm_forward(values, gain, shift):
@@ -360,7 +365,7 @@
     final = (
         lax.psum(s0.astype(jnp.bfloat16), "dp").astype(jnp.float32),
         lax.psum(s1.astype(jnp.bfloat16), "dp").astype(jnp.float32),
-        lax.psum(s2.astype(jnp.bfloat16), "dp").astype(jnp.float32),
+        _keep_up_gates(s2.astype(jnp.bfloat16), "dp").astype(jnp.float32),
         lax.psum(s3.astype(jnp.bfloat16), "dp").astype(jnp.float32),
         lax.psum(s4.astype(jnp.bfloat16), "dp").astype(jnp.float32),
         lax.psum(s5.astype(jnp.bfloat16), "dp").astype(jnp.float32),

time: 1120 us -> 946 us (0.84)
  waiting for transfers between devices: 200 us -> 19 us
    reduce_scatter x1, waiting for transfers between devices: 114 us -> 0.01 us  [on_device(): lax.psum_scatter(p11, 'fsdp', scatter_dimension=0, tiled=True)]
    reduce_scatter x1, waiting for transfers between devices: 52.8 us -> 0.01 us  [on_device(): lax.psum_scatter(p9, 'fsdp', scatter_dimension=0, tiled=True)]
    psum x1, waiting for transfers between devices: 30.7 us -> 16.3 us  [on_device(): lax.psum(s5.astype(jnp.bfloat16), 'dp').astype(jnp.float32)]
    unnamed x270 -> x278, local copies, waits for them, and re-layouts: 34.5 us -> 35.7 us
  transfers between devices with their start and end apart: 9 -> 9, of which waited for: 3 -> 1; matrix products, arithmetic and copies ran while one was open for 39% -> 65% of each run, Pallas kernels for 0% -> 0%
where the time goes in v1:
time: 946 us; the launch traced here: 935 us
  matrix products  504 us (53%)
  other arithmetic  191 us (20%)
  blocking collectives  138 us (15%)
  local copies, waits for them, and re-layouts  62.6 us (7%)
  waiting for transfers between devices  19 us (2%)
  between operations  18.4 us (2%)
    unnamed x2, blocking collectives  123 us
    dot_general x4, matrix products, attend_backward(): jnp.einsum('qhd,khd->hqk', grad_block, value, preferred_element_type=jnp....  86.8 us
    convert_element_type x4, other arithmetic, attend_backward(): grad_scores = (soft * (grad_soft - center)).astype(jnp.bfloat16)  76.7 us
    dot_general x2, matrix products, layer_forward(): jnp.dot(second_in, up_weight, preferred_element_type=jnp.float32)  72.6 us
    reduce_sum x4, other arithmetic, attend_forward(): total = jnp.sum(exponent, axis=-1, keepdims=True)  50.7 us
    dot_general x4, matrix products, masked_scores(): jnp.einsum('qhd,khd->hqk', query_block, keys, preferred_element_type=jnp....  48.8 us
    dot_general x4, matrix products, attend_backward(): jnp.einsum('hqk,qhd->khd', soft.astype(jnp.bfloat16), grad_block, preferr...  47.4 us
    unnamed x278, local copies, waits for them, and re-layouts  35.7 us
  transfers between devices with their start and end apart: 9, of which 1 were waited for; matrix products, arithmetic and copies ran while one was open for 65% of the time, Pallas kernels for 0%

profile of v1, /device:TPU:0, one launch (start us, length us, event | category | flops | bytes accessed | tf_op | source)
XLA Modules:
  0.0 934.5 jit_solution(5794656785630088483)
XLA Ops:
  21.7 63.5 %all-reduce.19 = (bf16[768]{0:T(1024)(128)(2,1)S(1)}, bf16[768]{0:T(1024)(128)(2,1)S(1)}, bf16[768]{0:T(1024)(128)(2,1)S(1)}, bf16[768]{0:T(1024)(128)(2,1)S(1)}...) all-reduce(bf16[768]{0:T(1024)(128)(2,1)S(1)} %dynamic-update-slice, ...), channel_id=1, replica_groups=mesh['dp'=2,'fsdp'=16] {'fsdp'}, use_global_device_ids=true, to_apply=%add.1 | all-reduce | flops 9216 | bytes 36864
  144.7 12.3 %fusion.55 = (f32[12,512]{1,0:T(8,128)S(1)}, f32[12,512,1024]{2,1,0:T(8,128)}) fusion(pred[512,1024]{1,0:T(8,128)(4,1)} %get-tuple-element.150, bf16[512,12,64]{0,2,1:T(8,128)(2,1)} %bitcast.137, bf16[1024,12,64]{0,2,1:T(8,128)(2,1)S(1)} %bitcast.119), kind=kOutput, calls=%fused_computation.95 | convolution fusion | flops 824174592 | bytes 28073984 | tf_op jit(solution)/shard_map/qhd,khd->hqk/dot_general | solution.py:45
  157.0 12.5 %fusion.1 = f32[12,512]{1,0:T(8,128)S(1)} fusion(f32[12,512]{1,0:T(8,128)S(1)} %get-tuple-element.121, f32[12,512,1024]{2,1,0:T(8,128)} %get-tuple-element.122, pred[512,1024]{1,0:T(8,128)(4,1)} %get-tuple-element.150), kind=kLoop, calls=%fused_computation.25 | loop fusion | flops 25159680 | bytes 25739264 | tf_op jit(solution)/shard_map/reduce_sum | solution.py:62
  182.7 12.2 %fusion.54 = (f32[12,512]{1,0:T(8,128)S(1)}, f32[12,512,1024]{2,1,0:T(8,128)}) fusion(pred[512,1024]{1,0:T(8,128)(4,1)} %get-tuple-element.151, bf16[512,12,64]{0,2,1:T(8,128)(2,1)} %bitcast.141, bf16[1024,12,64]{0,2,1:T(8,128)(2,1)S(1)} %bitcast.120), kind=kOutput, calls=%fused_computation.94 | convolution fusion | flops 824174592 | bytes 28073984 | tf_op jit(solution)/shard_map/qhd,khd->hqk/dot_general | solution.py:45
  194.9 13.6 %fusion = f32[12,512]{1,0:T(8,128)S(1)} fusion(f32[12,512]{1,0:T(8,128)S(1)} %get-tuple-element.123, f32[12,512,1024]{2,1,0:T(8,128)} %get-tuple-element.124, pred[512,1024]{1,0:T(8,128)(4,1)} %get-tuple-element.151), kind=kLoop, calls=%fused_computation.24 | loop fusion | flops 25159680 | bytes 25739264 | tf_op jit(solution)/shard_map/reduce_sum | solution.py:62
  219.8 12.2 %fusion.57 = (f32[12,512]{1,0:T(8,128)S(1)}, f32[12,512,1024]{2,1,0:T(8,128)}) fusion(pred[512,1024]{1,0:T(8,128)(4,1)S(1)} %copy-done.25, bf16[512,12,64]{0,2,1:T(8,128)(2,1)} %bitcast.135, bf16[1024,12,64]{0,2,1:T(8,128)(2,1)S(1)} %bitcast.123), kind=kOutput, calls=%fused_computation.97 | convolution fusion | flops 824174592 | bytes 28073984 | tf_op jit(solution)/shard_map/qhd,khd->hqk/dot_general | solution.py:45
  232.0 12.3 %fusion.3 = f32[12,512]{1,0:T(8,128)S(1)} fusion(f32[12,512]{1,0:T(8,128)S(1)} %get-tuple-element.117, f32[12,512,1024]{2,1,0:T(8,128)} %get-tuple-element.118, pred[512,1024]{1,0:T(8,128)(4,1)S(1)} %copy-done.25), kind=kLoop, calls=%fused_computation.27 | loop fusion | flops 25159680 | bytes 25739264 | tf_op jit(solution)/shard_map/reduce_sum | solution.py:62
  255.9 12.1 %fusion.56 = (f32[12,512]{1,0:T(8,128)S(1)}, f32[12,512,1024]{2,1,0:T(8,128)}) fusion(pred[512,1024]{1,0:T(8,128)(4,1)S(1)} %copy-done.22, bf16[512,12,64]{0,2,1:T(8,128)(2,1)} %bitcast.139, bf16[1024,12,64]{0,2,1:T(8,128)(2,1)S(1)} %bitcast.124), kind=kOutput, calls=%fused_computation.96 | convolution fusion | flops 824174592 | bytes 28073984 | tf_op jit(solution)/shard_map/qhd,khd->hqk/dot_general | solution.py:45
  267.9 12.3 %fusion.2 = f32[12,512]{1,0:T(8,128)S(1)} fusion(f32[12,512]{1,0:T(8,128)S(1)} %get-tuple-element.119, f32[12,512,1024]{2,1,0:T(8,128)} %get-tuple-element.120, pred[512,1024]{1,0:T(8,128)(4,1)S(1)} %copy-done.22), kind=kLoop, calls=%fused_computation.26 | loop fusion | flops 25159680 | bytes 25739264 | tf_op jit(solution)/shard_map/reduce_sum | solution.py:62
  304.5 11.0 %fusion.153 = f32[1024,3072]{1,0:T(8,128)} fusion(bf16[768,3072]{1,0:T(8,128)(2,1)} %all-gather.10.cloned.1.call-done, f32[1024,768]{1,0:T(8,128)} %copy-done.13, f32[1024]{0:T(1024)S(1)} %add_rsqrt_fusion, f32[1024]{0:T(1024)S(1)} %broadcast_multiply_fusion.8, f32[768]{0:T(1024)S(1)} %copy-done.66, f32[768]{0:T(1024)S(1)} %copy-done.65), kind=kOutput, calls=%fused_computation.276 | convolution fusion | flops 4835770368 | bytes 20461568 | tf_op jit(solution)/shard_map/dot_general | solution.py:152
  315.6 13.5 %fusion.166 = (f32[3072]{0:T(1024)}, bf16[1024,3072]{1,0:T(8,128)(2,1)S(1)}) fusion(f32[1024,3072]{1,0:T(8,128)} %fusion.153, f32[3072]{0:T(1024)S(1)} %copy-done.95, bf16[3072,768]{1,0:T(8,128)(2,1)} %all-gather.12.cloned.1.call-done, bf16[2048,768]{1,0:T(8,128)(2,1)} %param.17), kind=kOutput, calls=%fused_computation.289 | convolution fusion | flops 4869583872 | bytes 25190400 | tf_op jit(solution)/shard_map/rd,fd->rf/dot_general | solution.py:215
  335.9 61.6 %fusion.10 = (bf16[1024,3072]{1,0:T(8,128)(2,1)}, bf16[1024,3072]{1,0:T(8,128)(2,1)}, f32[1024,3072]{1,0:T(8,128)}) fusion(f32[3072]{0:T(1024)S(1)} %copy-done.95, f32[1024,3072]{1,0:T(8,128)S(1)} %bitcast.173, bf16[768,3072]{1,0:T(8,128)(2,1)S(1)} %copy-done.106, f32[1024,768]{1,0:T(8,128)S(1)} %get-tuple-element.126, f32[768]{0:T(1024)S(1)} %copy-done.66, ...), kind=kOutput, calls=%fused_computation.38 | convolution fusion | flops 5251006464 | bytes 45639680 | tf_op jit(solution)/shard_map/dot_general | solution.py:152
  397.5 12.0 %fusion.165 = (f32[3072]{0:T(1024)}, bf16[1024,3072]{1,0:T(8,128)(2,1)S(1)}) fusion(f32[1024,3072]{1,0:T(8,128)} %get-tuple-element.129, f32[3072]{0:T(1024)S(1)} %copy-done.95, bf16[3072,768]{1,0:T(8,128)(2,1)} %all-gather.12.cloned.1.call-done, bf16[2048,768]{1,0:T(8,128)(2,1)S(1)} %copy-done.48), kind=kOutput, calls=%fused_computation.288 | convolution fusion | flops 4869583872 | bytes 25190400 | tf_op jit(solution)/shard_map/rd,fd->rf/dot_general | solution.py:215
  409.5 12.9 %multiply_reduce_fusion.5 = (f32[768]{0:T(1024)}, f32[1024]{0:T(1024)S(1)}, f32[1024]{0:T(1024)S(1)}, f32[768]{0:T(1024)}, f32[768]{0:T(1024)}, /*index=5*/f32[1...) fusion(f32[1024,768]{1,0:T(8,128)S(1)} %get-tuple-element.126, f32[1024]{0:T(1024)S(1)} %add_rsqrt_fusion.2, ...), kind=kOutput, calls=%fused_computation.160 | convolution fusion | flops 4845985792 | bytes 23641088 | tf_op jit(solution)/shard_map/rf,df->rd/dot_general | solution.py:222
  447.1 11.3 %convolution_add_fusion.2 = f32[768,3072]{1,0:T(8,128)} fusion(f32[768,3072]{1,0:T(8,128)S(1)} %fusion.97, bf16[1024,3072]{1,0:T(8,128)(2,1)} %copy-done.40, f32[1024,768]{1,0:T(8,128)S(1)} %copy-done.15, f32[1024]{0:T(1024)S(1)} %copy-done.78, f32[1024]{0:T(1024)S(1)} %copy-done.68, f32[768]{0:T(1024)S(1)} %copy-done.66, f32[768]{0:T(1024)S(1)} %copy-done.65), kind=kOutput, calls=%fused_computation.100 | convolution fusion | flops 4838129664 | bytes 28325888 | tf_op jit(solution)/shard_map/rd,rf->df/dot_general | solution.py:219
  460.2 21.5 %multiply_reduce_fusion.1 = (f32[12,512]{1,0:T(8,128)S(1)}, f32[12,512,1024]{2,1,0:T(8,128)}) fusion(f32[12,512]{1,0:T(8,128)S(1)} %copy-done.69, f32[12,512,1024]{2,1,0:T(8,128)} %get-tuple-element.120, pred[512,1024]{1,0:T(8,128)(4,1)S(1)} %copy-done.23, bf16[512,12,64]{0,2,1:T(8,128)(2,1)S(1)} %bitcast.151, bf16[1024,12,64]{0,2,1:T(8,128)(2,1)S(1)} %bitcast.134), kind=kOutput, calls=%fused_computation.4 | convolution fusion | flops 836757504 | bytes 53264384 | tf_op jit(solution)/shard_map/qhd,khd->hqk/dot_general | solution.py:82
  481.8 17.3 %multiply_convert_fusion.1 = bf16[12,512,1024]{2,1,0:T(8,128)(2,1)S(1)} fusion(f32[12,512,1024]{2,1,0:T(8,128)} %get-tuple-element.136, f32[12,512]{1,0:T(8,128)S(1)} %get-tuple-element.135, f32[12,512]{1,0:T(8,128)S(1)} %copy-done.69, f32[12,512,1024]{2,1,0:T(8,128)} %get-tuple-element.120, pred[512,1024]{1,0:T(8,128)(4,1)} %get-tuple-element.113), kind=kLoop, calls=%fused_computation.3 | loop fusion | flops 37748736 | bytes 63488000 | tf_op jit(solution)/shard_map/convert_element_type | solution.py:86
  506.6 20.6 %multiply_reduce_fusion = (f32[12,512]{1,0:T(8,128)S(1)}, f32[12,512,1024]{2,1,0:T(8,128)}) fusion(f32[12,512]{1,0:T(8,128)S(1)} %copy-done.71, f32[12,512,1024]{2,1,0:T(8,128)} %get-tuple-element.118, pred[512,1024]{1,0:T(8,128)(4,1)} %get-tuple-element.114, bf16[512,12,64]{0,2,1:T(8,128)(2,1)} %bitcast.153, bf16[1024,12,64]{0,2,1:T(8,128)(2,1)} %bitcast.131), kind=kOutput, calls=%fused_computation.1 | convolution fusion | flops 836757504 | bytes 53264384 | tf_op jit(solution)/shard_map/qhd,khd->hqk/dot_general | solution.py:82
  527.2 18.3 %multiply_convert_fusion = bf16[12,512,1024]{2,1,0:T(8,128)(2,1)S(1)} fusion(f32[12,512,1024]{2,1,0:T(8,128)} %get-tuple-element.138, f32[12,512]{1,0:T(8,128)S(1)} %get-tuple-element.137, f32[12,512]{1,0:T(8,128)S(1)} %copy-done.71, f32[12,512,1024]{2,1,0:T(8,128)} %get-tuple-element.118, pred[512,1024]{1,0:T(8,128)(4,1)} %get-tuple-element.114), kind=kLoop, calls=%fused_computation | loop fusion | flops 37748736 | bytes 63488000 | tf_op jit(solution)/shard_map/convert_element_type | solution.py:86
  561.4 10.6 %convolution_add_fusion.1 = f32[3072,768]{1,0:T(8,128)} fusion(f32[3072,768]{1,0:T(8,128)S(1)} %fusion.118, bf16[1024,3072]{1,0:T(8,128)(2,1)} %get-tuple-element.98, bf16[2048,768]{1,0:T(8,128)(2,1)S(1)} %copy-done.49), kind=kOutput, calls=%fused_computation.99 | convolution fusion | flops 4834197504 | bytes 26738688 | tf_op jit(solution)/shard_map/rf,rd->fd/dot_general | solution.py:214
  573.8 21.7 %multiply_reduce_fusion.3 = (f32[12,512]{1,0:T(8,128)S(1)}, f32[12,512,1024]{2,1,0:T(8,128)}) fusion(f32[12,512]{1,0:T(8,128)S(1)} %copy-done.73, f32[12,512,1024]{2,1,0:T(8,128)} %get-tuple-element.124, pred[512,1024]{1,0:T(8,128)(4,1)S(1)} %copy-done.28, bf16[512,12,64]{0,2,1:T(8,128)(2,1)S(1)} %bitcast.155, bf16[1024,12,64]{0,2,1:T(8,128)(2,1)S(1)} %bitcast.129), kind=kOutput, calls=%fused_computation.10 | convolution fusion | flops 836757504 | bytes 53264384 | tf_op jit(solution)/shard_map/qhd,khd->hqk/dot_general | solution.py:82
  595.5 22.1 %multiply_convert_fusion.3 = bf16[12,512,1024]{2,1,0:T(8,128)(2,1)} fusion(f32[12,512,1024]{2,1,0:T(8,128)} %get-tuple-element.132, f32[12,512]{1,0:T(8,128)S(1)} %get-tuple-element.131, f32[12,512]{1,0:T(8,128)S(1)} %copy-done.73, f32[12,512,1024]{2,1,0:T(8,128)} %get-tuple-element.124, pred[512,1024]{1,0:T(8,128)(4,1)S(1)} %copy-done.28), kind=kLoop, calls=%fused_computation.9 | loop fusion | flops 37748736 | bytes 63488000 | tf_op jit(solution)/shard_map/convert_element_type | solution.py:86
  617.6 22.9 %multiply_reduce_fusion.2 = (f32[12,512]{1,0:T(8,128)S(1)}, f32[12,512,1024]{2,1,0:T(8,128)}) fusion(f32[12,512]{1,0:T(8,128)S(1)} %copy-done.74, f32[12,512,1024]{2,1,0:T(8,128)} %get-tuple-element.122, pred[512,1024]{1,0:T(8,128)(4,1)S(1)} %copy-done.30, bf16[512,12,64]{0,2,1:T(8,128)(2,1)S(1)} %bitcast.157, bf16[1024,12,64]{0,2,1:T(8,128)(2,1)S(1)} %bitcast.130), kind=kOutput, calls=%fused_computation.7 | convolution fusion | flops 836757504 | bytes 53264384 | tf_op jit(solution)/shard_map/qhd,khd->hqk/dot_general | solution.py:82
  640.5 19.0 %multiply_convert_fusion.2 = bf16[12,512,1024]{2,1,0:T(8,128)(2,1)S(1)} fusion(f32[12,512,1024]{2,1,0:T(8,128)} %get-tuple-element.134, f32[12,512]{1,0:T(8,128)S(1)} %get-tuple-element.133, f32[12,512]{1,0:T(8,128)S(1)} %copy-done.74, f32[12,512,1024]{2,1,0:T(8,128)} %get-tuple-element.122, pred[512,1024]{1,0:T(8,128)(4,1)} %get-tuple-element.150), kind=kLoop, calls=%fused_computation.6 | loop fusion | flops 37748736 | bytes 63488000 | tf_op jit(solution)/shard_map/convert_element_type | solution.py:86
  704.2 11.5 %fusion.28 = f32[12,64,1024]{2,1,0:T(8,128)S(1)} fusion(bf16[512,12,64]{0,2,1:T(8,128)(2,1)S(1)} %bitcast.158, f32[12,512]{1,0:T(8,128)S(1)} %copy-done.74, f32[12,512,1024]{2,1,0:T(8,128)} %get-tuple-element.122, pred[512,1024]{1,0:T(8,128)(4,1)S(1)} %copy-done.31), kind=kOutput, calls=%fused_computation.54 | convolution fusion | flops 830472192 | bytes 29646848 | tf_op jit(solution)/shard_map/hqk,qhd->khd/dot_general | solution.py:98
  715.9 12.2 %convert_reduce_fusion.5 = (f32[12,64]{1,0:T(8,128)S(1)}, bf16[12,64,1024]{2,1,0:T(8,128)(2,1)S(1)}) fusion(f32[12,64,1024]{2,1,0:T(8,128)S(1)} %fusion.28, bf16[512,12,64]{0,2,1:T(8,128)(2,1)S(1)} %bitcast.156, f32[12,512]{1,0:T(8,128)S(1)} %copy-done.73, f32[12,512,1024]{2,1,0:T(8,128)} %get-tuple-element.124, pred[512,1024]{1,0:T(8,128)(4,1)S(1)} %copy-done.29), kind=kOutput, calls=%fused_computation.162 | convolution fusion | flops 833617152 | bytes 31222784 | tf_op jit(solution)/shard_map/hqk,qhd->khd/dot_general | solution.py:98
  736.5 11.7 %fusion.24 = f32[12,64,1024]{2,1,0:T(8,128)S(1)} fusion(bf16[512,12,64]{0,2,1:T(8,128)(2,1)S(1)} %bitcast.154, f32[12,512]{1,0:T(8,128)S(1)} %copy-done.72, f32[12,512,1024]{2,1,0:T(8,128)} %get-tuple-element.118, pred[512,1024]{1,0:T(8,128)(4,1)S(1)} %copy-done.26), kind=kOutput, calls=%fused_computation.52 | convolution fusion | flops 830472192 | bytes 29646848 | tf_op jit(solution)/shard_map/hqk,qhd->khd/dot_general | solution.py:98
  748.3 12.0 %convert_reduce_fusion.4 = (f32[12,64]{1,0:T(8,128)S(1)}, bf16[12,64,1024]{2,1,0:T(8,128)(2,1)S(1)}) fusion(f32[12,64,1024]{2,1,0:T(8,128)S(1)} %fusion.24, bf16[512,12,64]{0,2,1:T(8,128)(2,1)S(1)} %bitcast.152, f32[12,512]{1,0:T(8,128)S(1)} %copy-done.70, f32[12,512,1024]{2,1,0:T(8,128)} %get-tuple-element.120, pred[512,1024]{1,0:T(8,128)(4,1)S(1)} %copy-done.24), kind=kOutput, calls=%fused_computation.161 | convolution fusion | flops 833617152 | bytes 31222784 | tf_op jit(solution)/shard_map/hqk,qhd->khd/dot_general | solution.py:98
  761.5 10.2 %convolution_add_fusion = f32[768,2304]{1,0:T(8,128)} fusion(f32[768,2304]{1,0:T(8,128)} %fusion.102, bf16[1024,768]{0,1:T(8,128)(2,1)S(1)} %bitcast.170, bf16[1024,768]{0,1:T(8,128)(2,1)S(1)} %bitcast.150, bf16[1024,768]{0,1:T(8,128)(2,1)S(1)} %bitcast.163, f32[1024]{0:T(1024)S(1)} %copy-done.94, f32[1024]{0:T(1024)S(1)} %copy-done.82, ...), kind=kOutput, calls=%fused_computation.98 | convolution fusion | flops 3644522496 | bytes 20463616 | tf_op jit(solution)/shard_map/rd,re->de/dot_general | solution.py:244
  789.4 59.6 %all-reduce.18 = (bf16[768]{0:T(1024)(128)(2,1)S(1)}, bf16[768]{0:T(1024)(128)(2,1)S(1)}, bf16[768]{0:T(1024)(128)(2,1)S(1)}, bf16[768]{0:T(1024)(128)(2,1)S(1)}...) all-reduce(f32[768]{0:T(1024)S(1)} %add.385, ...), channel_id=16, replica_groups=mesh['dp'=2,'fsdp'=16] {'fsdp'}, use_global_device_ids=true, to_apply=%region_29.30.clone | all-reduce | flops 9216 | bytes 55296
  866.5 10.3 %add_convert_fusion.4 = bf16[1024,768]{1,0:T(8,128)(2,1)} fusion(f32[1024,768]{1,0:T(8,128)S(1)} %copy-done.9, bf16[1024,3072]{1,0:T(8,128)(2,1)} %get-tuple-element.97, bf16[3072,768]{1,0:T(8,128)(2,1)} %all-gather.12.cloned.1.call-done, f32[768]{0:T(1024)S(1)} %convert_element_type.329), kind=kOutput, calls=%fused_computation.181 | convolution fusion | flops 4834197504 | bytes 15731712 | tf_op jit(solution)/shard_map/dot_general | solution.py:158
  906.1 16.3 %all-reduce.24.cloned.1.call-done = (bf16[48,768]{1,0:T(8,128)(2,1)}, bf16[48,3072]{1,0:T(8,128)(2,1)}, bf16[192,768]{1,0:T(8,128)(2,1)}) async-done(((bf16[48,768]{1,0:T(8,128)(2,1)}, bf16[48,3072]{1,0:T(8,128)(2,1)}, bf16[192,768]{1,0:T(8,128)(2,1)}), (bf16[48,768]{1,0:T(8,128)(2,1)}, bf16[48,3072]{1,0:T(8,128)(2,1)}, bf16[192,768]{1,0:T(8,128)(2,1)})) %all-reduce.24.cloned.1.call-update) | async-done | bytes 663568 | tf_op jit(solution)/shard_map/psum | solution.py:371
  (425 shorter events, 313.0 us)
Async XLA Ops:
  7.2 82.3 %copy-start.10 = (bf16[2048,768]{1,0:T(8,128)(2,1)S(1)}, bf16[2048,768]{1,0:T(8,128)(2,1)}, u32[]{:S(2)}) copy-start(bf16[2048,768]{1,0:T(8,128)(2,1)} %param.16) | copy-start | bytes 9437188
  7.2 86.3 %all-gather.6.cloned.1.call-start = ((), (), s32[]{:S(2)}) async-start(), calls=%async_computation.4 | async-start | bytes 3760128 | tf_op jit(solution)/shard_map/all_gather | solution.py:314
  7.9 285.6 %all-gather.8.cloned.1.call-start = ((), (), s32[]{:S(2)}) async-start(), calls=%async_computation.5 | async-start | bytes 1253376 | tf_op jit(solution)/shard_map/all_gather | solution.py:317
  8.7 295.9 %all-gather.10.cloned.1.call-start = ((), (), s32[]{:S(2)}) async-start(), calls=%async_computation.6 | async-start | bytes 5013504 | tf_op jit(solution)/shard_map/all_gather | solution.py:321
  9.4 306.1 %all-gather.12.cloned.1.call-start = ((), (), s32[]{:S(2)}) async-start(), calls=%async_computation.7 | async-start | bytes 5013504 | tf_op jit(solution)/shard_map/all_gather | solution.py:323
  10.0 873.0 %reduce-scatter.7.cloned.1.call-start = ((), (), s32[]{:S(2)}) async-start(), calls=%async_computation.9 | async-start | bytes 2506752 | tf_op jit(solution)/shard_map/reduce_scatter | solution.py:354
  85.2 19.0 %copy-start.102 = (f32[768]{0:T(1024)}, f32[768]{0:T(1024)S(1)}, u32[]{:S(2)}) copy-start(f32[768]{0:T(1024)S(1)} %convert_element_type.314) | copy-start | bytes 9220
  85.2 19.0 %copy-start.89 = (f32[768]{0:T(1024)}, f32[768]{0:T(1024)S(1)}, u32[]{:S(2)}) copy-start(f32[768]{0:T(1024)S(1)} %convert_element_type.313) | copy-start | bytes 9220
  104.3 151.5 %copy-start.7 = (bf16[1024,768]{0,1:T(8,128)(2,1)}, bf16[1024,768]{0,1:T(8,128)(2,1)S(1)}, u32[]{:S(2)}) copy-start(bf16[1024,768]{0,1:T(8,128)(2,1)S(1)} %copy.69) | copy-start | bytes 4718596
  118.1 64.6 %copy-start.6 = (bf16[1024,768]{0,1:T(8,128)(2,1)}, bf16[1024,768]{0,1:T(8,128)(2,1)S(1)}, u32[]{:S(2)}) copy-start(bf16[1024,768]{0,1:T(8,128)(2,1)S(1)} %copy.65) | copy-start | bytes 4718596
  144.7 24.9 %copy-start.18 = (bf16[1024,768]{0,1:T(8,128)(2,1)S(1)}, bf16[1024,768]{0,1:T(8,128)(2,1)}, u32[]{:S(2)}) copy-start(bf16[1024,768]{0,1:T(8,128)(2,1)} %copy.63) | copy-start | bytes 4718596
  157.0 16.2 %copy-start.3 = (f32[12,512,1024]{2,1,0:T(8,128)S(1)}, f32[12,512,1024]{2,1,0:T(8,128)}, u32[]{:S(2)}) copy-start(f32[12,512,1024]{2,1,0:T(8,128)} %get-tuple-element.122) | copy-start | bytes 75497472
  194.9 16.3 %copy-start.2 = (f32[12,512,1024]{2,1,0:T(8,128)S(1)}, f32[12,512,1024]{2,1,0:T(8,128)}, u32[]{:S(2)}) copy-start(f32[12,512,1024]{2,1,0:T(8,128)} %get-tuple-element.124) | copy-start | bytes 75497472
  194.9 16.4 %copy-start.27 = (pred[512,1024]{1,0:T(8,128)(4,1)S(1)}, pred[512,1024]{1,0:T(8,128)(4,1)}, u32[]{:S(2)}) copy-start(pred[512,1024]{1,0:T(8,128)(4,1)} %get-tuple-element.151) | copy-start | bytes 1572868
  219.8 24.5 %copy-start.20 = (bf16[1024,768]{0,1:T(8,128)(2,1)S(1)}, bf16[1024,768]{0,1:T(8,128)(2,1)}, u32[]{:S(2)}) copy-start(bf16[1024,768]{0,1:T(8,128)(2,1)} %copy.67) | copy-start | bytes 4718596
  255.9 24.4 %copy-start.63 = (bf16[512,12,64]{0,2,1:T(8,128)(2,1)S(1)}, bf16[512,12,64]{0,2,1:T(8,128)(2,1)}, u32[]{:S(2)}) copy-start(bf16[512,12,64]{0,2,1:T(8,128)(2,1)} %fusion.113) | copy-start | bytes 2359300
  267.9 16.1 %copy-start.1 = (f32[12,512,1024]{2,1,0:T(8,128)S(1)}, f32[12,512,1024]{2,1,0:T(8,128)}, u32[]{:S(2)}) copy-start(f32[12,512,1024]{2,1,0:T(8,128)} %get-tuple-element.120) | copy-start | bytes 75497472
  297.5 143.9 %copy-start.8 = (f32[1024,768]{1,0:T(8,128)}, f32[1024,768]{1,0:T(8,128)S(1)}, u32[]{:S(2)}) copy-start(f32[1024,768]{1,0:T(8,128)S(1)} %get-tuple-element.126) | copy-start | bytes 9437188
  315.6 20.3 %slice-start.7 = ((s8[12582912]{0:T(1024)(128)(4,1)}), s8[4194304]{0:T(1024)(128)(4,1)S(1)}, s32[]{:S(2)}) async-start(s8[12582912]{0:T(1024)(128)(4,1)} %bitcast.172), calls=%async_computation.20 | async-start | bytes 8388608
  315.6 20.3 %slice-start.8 = ((s8[12582912]{0:T(1024)(128)(4,1)}), s8[4194304]{0:T(1024)(128)(4,1)S(1)}, s32[]{:S(2)}) async-start(s8[12582912]{0:T(1024)(128)(4,1)} %bitcast.172), calls=%async_computation.21 | async-start | bytes 8388608
  335.8 61.7 %copy-start.48 = (bf16[2048,768]{1,0:T(8,128)(2,1)S(1)}, bf16[2048,768]{1,0:T(8,128)(2,1)}, u32[]{:S(2)}) copy-start(bf16[2048,768]{1,0:T(8,128)(2,1)} %param.17) | copy-start | bytes 9437188
  433.4 451.3 %reduce-scatter.9.cloned.1.call-start = ((), (), s32[]{:S(2)}) async-start(), calls=%async_computation.10 | async-start | bytes 10027008 | tf_op jit(solution)/shard_map/reduce_scatter | solution.py:358
  458.4 428.1 %reduce-scatter.11.cloned.1.call-start = ((), (), s32[]{:S(2)}) async-start(), calls=%async_computation.11 | async-start | bytes 10027008 | tf_op jit(solution)/shard_map/reduce_scatter | solution.py:360
  572.0 321.9 %reduce-scatter.5.cloned.1.call-start = ((), (), s32[]{:S(2)}) async-start(), calls=%async_computation.8 | async-start | bytes 7520256 | tf_op jit(solution)/shard_map/reduce_scatter | solution.py:351
  595.5 22.1 %copy-start.30 = (pred[512,1024]{1,0:T(8,128)(4,1)S(1)}, pred[512,1024]{1,0:T(8,128)(4,1)}, u32[]{:S(2)}) copy-start(pred[512,1024]{1,0:T(8,128)(4,1)} %get-tuple-element.150) | copy-start | bytes 1572868
  595.5 22.1 %copy-start.57 = (bf16[512,768]{0,1:T(8,128)(2,1)S(1)}, bf16[512,768]{0,1:T(8,128)(2,1)}, u32[]{:S(2)}) copy-start(bf16[512,768]{0,1:T(8,128)(2,1)} %get-tuple-element.90) | copy-start | bytes 2359300
  595.5 22.1 %copy-start.74 = (f32[12,512]{1,0:T(8,128)S(1)}, f32[12,512]{1,0:T(8,128)}, u32[]{:S(2)}) copy-start(f32[12,512]{1,0:T(8,128)} %log_add_fusion.2) | copy-start | bytes 73732
  640.5 19.0 %copy-start.46 = (bf16[512,12,64]{0,2,1:T(8,128)(2,1)S(1)}, bf16[512,12,64]{0,2,1:T(8,128)(2,1)}, u32[]{:S(2)}) copy-start(bf16[512,12,64]{0,2,1:T(8,128)(2,1)} %multiply_bitcast_fusion.1) | copy-start | bytes 2359300
  640.5 19.0 %copy-start.47 = (bf16[512,12,64]{0,2,1:T(8,128)(2,1)S(1)}, bf16[512,12,64]{0,2,1:T(8,128)(2,1)}, u32[]{:S(2)}) copy-start(bf16[512,12,64]{0,2,1:T(8,128)(2,1)} %multiply_bitcast_fusion) | copy-start | bytes 2359300
  771.8 150.6 %all-reduce.24.cloned.1.call-start = ((), (), s32[]{:S(2)}) async-start(), calls=%async_computation.12 | async-start | bytes 1327104 | tf_op jit(solution)/shard_map/psum | solution.py:371
  859.3 17.4 %slice-start.5 = ((s8[4718592]{0:T(1024)(128)(4,1)}), s8[4194304]{0:T(1024)(128)(4,1)S(1)}, s32[]{:S(2)}) async-start(s8[4718592]{0:T(1024)(128)(4,1)} %bitcast.166), calls=%async_computation.18 | async-start | bytes 8388608
  859.4 17.4 %slice-start.10 = ((s8[6291456]{0:T(1024)(128)(4,1)}), s8[4194304]{0:T(1024)(128)(4,1)S(1)}, s32[]{:S(2)}) async-start(s8[6291456]{0:T(1024)(128)(4,1)} %bitcast.174), calls=%async_computation.23 | async-start | bytes 8388608
  (102 other events, 770.1 us)
Sparse Core Ops, SparseCore 0:
  10.3 49.9 all-gather.5
  62.6 37.2 all-gather.7
  102.2 52.1 all-gather.9
  156.5 51.7 all-gather.11
  433.5 60.1 reduce-scatter.6
  498.2 110.3 reduce-scatter.8
  612.6 111.1 reduce-scatter.10
  771.9 88.1 reduce-scatter.4
  888.5 33.8 all-reduce.23
